TPU v7x, 32 devices: a whole 2x2x4 slice. The times are simulated.
32 devices in a mesh: groups: 2 (over y), tile: 16 (over z, x, core).
Axes of the slice: x: 2, y: 2, z: 4, core: 2. Of those that a mesh axis runs over, the one named last changes fastest.
Arguments:
- features: bfloat16 [192, 16, 16, 256], P(('groups', 'tile')), parts along dimension 0, may hold values from -6 to 6
- weights: bfloat16 [9, 256, 256], replicated, may hold values from -0.125 to 0.125
- grad_out: bfloat16 [192, 16, 16, 256], P(('groups', 'tile')), parts along dimension 0, may hold values from -6 to 6
- tile_pos: int32 [192], P(('groups', 'tile')), parts along dimension 0, may hold values from -1 to 7, as said below
- neighbours: int32 [192, 8], P(('groups', 'tile')), parts along dimension 0, may hold values from -1 to 15, as said below
Outputs:
- activation: bfloat16 [192, 16, 16, 256], P(('groups', 'tile')), parts along dimension 0
- weight_grad: float32 [18, 256, 256], P('groups'), parts along dimension 0
- input_grad: bfloat16 [192, 16, 16, 256], P(('groups', 'tile')), parts along dimension 0
There are 2 independent parts, one for each index of `groups`. A program takes and returns all parts, laid end to end along the dimension named above; an argument that names none is the same for every part. Nothing has to cross between parts.
Inputs may be any that keep to these rules, and one draw needn't show every extreme that they name: `tile_pos`: each device's 6 slots hold the tissue tiles of its band of 2 x 4 tiles first, in raster order, then empty slots; every device holds 2 or more tissue tiles and at least one device holds 6. A code c names slot c % 6 of the device whose index is the own index plus c // 6 - 1; codes of left and right neighbours name the own device, up and up-diagonal neighbours lie on the own or the preceding device, down and down-diagonal ones on the own or the following device. Neighbours are tissue tiles of the slide's grid and the relation is symmetric; empty slots and missing neighbours have -1.
All inputs are finite; a program needn't handle non-finite values.
Results may differ from a plain program's by a relative error of at most 0.0049.
Values may be sent and summed in bfloat16 or wider, within the bound.
No kernel may reach another device: no remote copies, remote signals or barrier semaphores. Data moves between devices by JAX's collectives and lax.ppermute only.
A program may use at most 64 MiB of HBM per device.

v0:
```python
import math
import jax
import jax.numpy as jnp
from jax import lax
from jax.sharding import PartitionSpec as P

EDGE_PICK = (1, 0, 3, 2, 1, 1, 0, 0)
ROOT_HALF = 0.7071067811865476
INV_ROOT_TAU = 0.3989422804014327


def from_behind(value, axis, steps):
    count = lax.axis_size(axis)
    initial, last = (max(0, -steps), min(count, count - steps))
    return lax.ppermute(value, axis, [(source, source + steps) for source in range(initial, last)])


def gelu_value(preact):
    return preact * (0.5 * (1.0 + lax.erf(preact * ROOT_HALF)))


def gelu_slope(preact):
    cumulative = 0.5 * (1.0 + lax.erf(preact * ROOT_HALF))
    density = jnp.exp(-0.5 * preact * preact) * INV_ROOT_TAU
    return cumulative + preact * density


def edge_rims(field_map):
    return jnp.stack(
        [field_map[:, 0], field_map[:, -1], field_map[:, :, 0], field_map[:, :, -1]], axis=1
    )


def surround(center, gathered):
    upper_row = jnp.concatenate([gathered[:, 4, -1:], gathered[:, 0], gathered[:, 5, :1]], axis=1)
    lower_row = jnp.concatenate([gathered[:, 6, -1:], gathered[:, 1], gathered[:, 7, :1]], axis=1)
    middle = jnp.concatenate(
        [gathered[:, 2][:, :, None], center, gathered[:, 3][:, :, None]], axis=2
    )
    return jnp.concatenate([upper_row[:, None], middle, lower_row[:, None]], axis=1)


def tap_matrix(extended, flipped):
    side_cells = extended.shape[1] - 2
    pieces = []
    for row_tap in range(3):
        for col_tap in range(3):
            row_start = 2 - row_tap if flipped else row_tap
            col_start = 2 - col_tap if flipped else col_tap
            pieces.append(
                extended[:, row_start : row_start + side_cells, col_start : col_start + side_cells]
            )
    stacked = jnp.concatenate(pieces, axis=-1)
    return stacked.reshape(-1, stacked.shape[-1])


def lookup(edge_table, source, linked):
    clipped = jnp.clip(jnp.where(linked, source, 0), 0, edge_table.shape[0] - 1)
    picked = jnp.take(edge_table, clipped.reshape(-1), axis=0).reshape(
        linked.shape + edge_table.shape[1:]
    )
    return jnp.where(linked[:, :, None, None], picked, jnp.zeros((), picked.dtype))


def narrow_sources(neighbours, edge_picks, tile_dev):
    anchor = neighbours // tile_dev
    own_slot = (neighbours - tile_dev) * 4 + edge_picks[None, :]
    return jnp.where(
        anchor == 1,
        own_slot,
        jnp.where(anchor == 0, 4 * tile_dev + neighbours, 3 * tile_dev + neighbours),
    )


def narrow_table(own_rims, upper_rows, lower_rows):
    tile_dev = own_rims.shape[0]
    side_cells = own_rims.shape[2]
    channels = own_rims.shape[3]
    return jnp.concatenate(
        [own_rims.reshape(4 * tile_dev, side_cells, channels), upper_rows, lower_rows], axis=0
    )


def forward_tiles(extended, grad_tiles, tissue_gate, weight_mat):
    tile_count = extended.shape[0]
    side_cells = extended.shape[1] - 2
    channels = weight_mat.shape[1]
    preact = jnp.dot(tap_matrix(extended, False), weight_mat, preferred_element_type=jnp.float32)
    preact = preact.reshape(tile_count, side_cells, side_cells, channels)
    gate_cells = tissue_gate[:, None, None, None]
    act_map = (gelu_value(preact) * gate_cells).astype(jnp.bfloat16)
    slope_map = (grad_tiles.astype(jnp.float32) * gelu_slope(preact) * gate_cells).astype(
        jnp.bfloat16
    )
    return (act_map, slope_map)


def weight_terms(ext_x, slope_map):
    return lax.dot_general(
        tap_matrix(ext_x, False),
        slope_map.reshape(-1, slope_map.shape[-1]),
        (((0,), (0,)), ((), ())),
        preferred_element_type=jnp.float32,
    )


def backward_tiles(ext_g, tissue_gate, flip_mat):
    tile_count = ext_g.shape[0]
    side_cells = ext_g.shape[1] - 2
    channels = flip_mat.shape[1]
    back_map = jnp.dot(tap_matrix(ext_g, True), flip_mat, preferred_element_type=jnp.float32)
    back_map = (
        back_map.reshape(tile_count, side_cells, side_cells, channels)
        * tissue_gate[:, None, None, None]
    )
    return back_map.astype(jnp.bfloat16)


def body(features, weights, grad_out, tile_pos, neighbours):
    tile_dev = features.shape[0]
    side_cells = features.shape[1]
    channels = features.shape[3]
    devices = lax.axis_size("tile")
    tissue = (tile_pos >= 0).astype(jnp.float32)
    weight_mat = weights.reshape(9 * channels, channels)
    flip_mat = jnp.transpose(weights, (0, 2, 1)).reshape(9 * channels, channels)
    edge_picks = jnp.array(EDGE_PICK, dtype=jnp.int32)
    linked = neighbours >= 0
    rims_x = edge_rims(features)
    from_above = from_behind(rims_x[:, 1], "tile", 1)
    from_below = from_behind(rims_x[:, 0], "tile", -1)
    table_x = narrow_table(rims_x, from_above, from_below)
    source = narrow_sources(neighbours, edge_picks, tile_dev)
    ext_x = surround(features, lookup(table_x, source, linked))
    activation, pre_grad = forward_tiles(ext_x, grad_out, tissue, weight_mat)
    rims_g = edge_rims(pre_grad)
    grad_above = from_behind(rims_g[:, 1], "tile", 1)
    grad_below = from_behind(rims_g[:, 0], "tile", -1)
    table_g = narrow_table(rims_g, grad_above, grad_below)
    ext_g = surround(pre_grad, lookup(table_g, source, linked))
    weight_part = weight_terms(ext_x, pre_grad)
    grad_scale = 1.0 / math.sqrt(tile_dev * devices * side_cells * side_cells)
    summed = lax.psum(weight_part, "tile")
    weight_grad = (summed * grad_scale).reshape(9, channels, channels)
    input_grad = backward_tiles(ext_g, tissue, flip_mat)
    return (activation, weight_grad, input_grad)


def solution(mesh):
    in_specs = (
        P(("groups", "tile"), None, None, None),
        P(),
        P(("groups", "tile"), None, None, None),
        P(("groups", "tile")),
        P(("groups", "tile"), None),
    )
    out_specs = (
        P(("groups", "tile"), None, None, None),
        P("groups", None, None),
        P(("groups", "tile"), None, None, None),
    )
    return jax.shard_map(body, mesh=mesh, in_specs=in_specs, out_specs=out_specs, check_vma=False)
```

profile of v0, /device:TPU:0, one launch (start us, length us, event | category | flops | bytes accessed | tf_op | source)
XLA Modules:
  0.0 143.3 jit_solution(6044019779046628402)
XLA Ops:
  7.2 0.0 copy-start.1
  7.2 0.0 all-reduce.2.cloned.1.call-start
  7.2 0.9 slice_bitcast_fusion.11
  8.2 1.3 collective-permute-start.1
  9.5 3.0 %collective-permute-start = (bf16[6,16,256]{2,1,0:T(8,128)(2,1)S(1)}, bf16[6,16,256]{2,1,0:T(8,128)(2,1)S(1)}, u32[]{:S(2)}, u32[]{:S(2)}) collective-permute-start(bf16[6,16,256]{2,1,0:T(8,128)(2,1)S(1)} %get-tuple-element.18), channel_id=1, source_target_pairs={{0,1},{1,2},{2,3},{3,4},{4,5},{5,6},{6,7},{7,8},{8,9},{9,10},{10,1... | collective-permute-start | bytes 147464 | tf_op jit(solution)/shard_map/ppermute | solution.py:15
  12.5 1.3 fusion.14
  13.8 0.7 select_clamp_fusion
  14.5 0.1 reshape.50
  14.6 0.7 broadcast_compare_fusion
  15.3 0.7 compare_convert_fusion
  16.0 0.1 copy.60
  16.1 0.0 copy-done.1
  16.1 1.6 %copy.89 = bf16[9,256,256]{1,2,0:T(8,128)(2,1)} copy(bf16[9,256,256]{2,1,0:T(8,128)(2,1)S(1)} %copy-done.1) | data formatting | bytes 2359296 | tf_op args[1]
  17.7 0.0 copy-start
  17.7 0.0 collective-permute-done.1
  17.7 0.0 collective-permute-done
  17.8 0.6 gather_fusion
  18.3 0.1 broadcast_select_fusion.1
  18.5 0.1 copy_select_fusion.1
  18.7 0.1 copy.70
  18.7 0.1 copy.69
  18.9 0.0 copy-done
  18.9 1.2 pad_maximum_fusion
  20.2 0.1 slice_dynamic-update-slice_fusion.11
  20.2 0.3 slice_dynamic-update-slice_fusion.10
  20.6 0.3 slice_dynamic-update-slice_fusion.9
  20.9 0.4 fusion.10
  21.2 0.1 constant_dynamic-update-slice_fusion
  21.3 0.5 fusion.9
  21.8 0.0 copy-start.3
  21.8 0.1 slice_dynamic-update-slice_fusion.8
  21.9 0.3 slice_dynamic-update-slice_fusion.7
  22.2 0.3 slice_dynamic-update-slice_fusion.6
  22.5 0.4 copy-done.3
  22.9 3.6 %fusion.6 = (bf16[6,16,16,256]{3,2,1,0:T(8,128)(2,1)S(1)}, bf16[6,16,16,256]{3,2,1,0:T(8,128)(2,1)}) fusion(bf16[6,16,16,256]{3,2,1,0:T(8,128)(2,1)S(1)} %copy-done.3, f32[6]{0:T(128)S(1)} %compare_convert_fusion, bf16[6,16,16,2304]{3,2,1,0:T(8,128)(2,1)S(1)} %slice_dynamic-update-slice_fusion.6, bf16[2304,256,1,1]{1,0,3,2:T(8,128)(2,1)S(1)} %bitcast.104), kind=kOutput, calls=%fused_computation.10 | convolution fusion | flops 1817837568 | bytes 10616856 | tf_op jit(solution)/shard_map/dot_general | solution.py:88
  26.5 3.5 %convolution_bitcast_fusion = f32[2304,256]{1,0:T(8,128)} fusion(bf16[6,16,16,2304]{3,2,1,0:T(8,128)(2,1)S(1)} %slice_dynamic-update-slice_fusion.6, bf16[6,16,16,256]{3,2,1,0:T(8,128)(2,1)S(1)} %get-tuple-element.4), kind=kOutput, calls=%fused_computation.2 | convolution fusion | flops 1811939328 | bytes 10223616 | tf_op jit(solution)/shard_map/dot_general | solution.py:99
  30.0 0.2 fusion.13
  30.2 0.0 all-reduce.2.cloned.1.call-update
  30.2 1.3 collective-permute-start.3
  31.5 5.3 %collective-permute-start.2 = (bf16[6,16,256]{2,1,0:T(8,128)(2,1)S(1)}, bf16[6,16,256]{2,1,0:T(8,128)(2,1)S(1)}, u32[]{:S(2)}, u32[]{:S(2)}) collective-permute-start(bf16[6,16,256]{2,1,0:T(8,128)(2,1)S(1)} %get-tuple-element.12), channel_id=1, source_target_pairs={{0,1},{1,2},{2,3},{3,4},{4,5},{5,6},{6,7},{7,8},{8,9},{9,10},{10,1... | collective-permute-start | bytes 147464 | tf_op jit(solution)/shard_map/ppermute | solution.py:15
  36.9 0.0 collective-permute-done.3
  36.9 0.6 collective-permute-done.2
  37.6 0.6 gather_fusion.1
  38.2 0.1 broadcast_select_fusion
  38.3 0.1 copy_select_fusion
  38.5 0.1 copy.80
  38.6 0.1 copy.79
  38.7 1.2 maximum_maximum_fusion.1
  39.9 0.3 slice_dynamic-update-slice_fusion.5
  40.2 0.3 slice_dynamic-update-slice_fusion.4
  40.5 0.1 slice_dynamic-update-slice_fusion.3
  40.6 0.5 fusion.8
  41.1 0.1 constant_dynamic-update-slice_fusion.1
  41.1 0.4 fusion.7
  41.5 0.0 copy-start.2
  41.5 0.3 slice_dynamic-update-slice_fusion.2
  41.8 0.3 slice_dynamic-update-slice_fusion.1
  42.2 0.1 slice_dynamic-update-slice_fusion
  42.2 0.5 copy-done.2
  42.8 3.0 %multiply_convert_fusion = bf16[6,16,16,256]{3,2,1,0:T(8,128)(2,1)} fusion(bf16[6,16,16,2304]{3,2,1,0:T(8,128)(2,1)S(1)} %slice_dynamic-update-slice_fusion, bf16[2304,256,1,1]{1,0,3,2:T(8,128)(2,1)S(1)} %bitcast.105, f32[6]{0:T(128)S(1)} %compare_convert_fusion), kind=kOutput, calls=%fused_computation.11 | convolution fusion | flops 1812725760 | bytes 9043992 | tf_op jit(solution)/shard_map/dot_general | solution.py:111
  45.7 87.5 %all-reduce.2.cloned.1.call-done = f32[2304,256]{1,0:T(8,128)} async-done(((f32[2304,256]{1,0:T(8,128)}), f32[2304,256]{1,0:T(8,128)}) %all-reduce.2.cloned.1.call-update) | async-done | bytes 2359312 | tf_op jit(solution)/shard_map/psum | solution.py:143
  133.2 3.3 %broadcast_multiply_fusion = f32[2304,256]{1,0:T(8,128)} fusion(f32[2304,256]{1,0:T(8,128)} %all-reduce.2.cloned.1.call-done), kind=kLoop, calls=%fused_computation.18 | loop fusion | flops 589824 | bytes 4718592 | tf_op jit(solution)/shard_map/mul | solution.py:144
  (20 shorter events, 0.4 us)
Async XLA Ops:
  7.2 9.0 %copy-start.1 = (bf16[9,256,256]{2,1,0:T(8,128)(2,1)S(1)}, bf16[9,256,256]{2,1,0:T(8,128)(2,1)}, u32[]{:S(2)}) copy-start(bf16[9,256,256]{2,1,0:T(8,128)(2,1)} %param.9) | copy-start | bytes 3538948
  7.2 126.0 %all-reduce.2.cloned.1.call-start = ((), (), s32[]{:S(2)}) async-start(), calls=%async_computation | async-start | bytes 4718592 | tf_op jit(solution)/shard_map/psum | solution.py:143
  8.2 9.6 %collective-permute-start.1 = (bf16[6,16,256]{2,1,0:T(8,128)(2,1)S(1)}, bf16[6,16,256]{2,1,0:T(8,128)(2,1)S(1)}, u32[]{:S(2)}, u32[]{:S(2)}) collective-permute-start(bf16[6,16,256]{2,1,0:T(8,128)(2,1)S(1)} %get-tuple-element.17), channel_id=1, source_target_pairs={{1,0},{2,1},{3,2},{4,3},{5,4},{6,5},{7,6},{8,7},{9,8},{10,9},{11,1... | collective-permute-start | bytes 147464 | tf_op jit(solution)/shard_map/ppermute | solution.py:15
  9.5 8.3 %collective-permute-start = (bf16[6,16,256]{2,1,0:T(8,128)(2,1)S(1)}, bf16[6,16,256]{2,1,0:T(8,128)(2,1)S(1)}, u32[]{:S(2)}, u32[]{:S(2)}) collective-permute-start(bf16[6,16,256]{2,1,0:T(8,128)(2,1)S(1)} %get-tuple-element.18), channel_id=1, source_target_pairs={{0,1},{1,2},{2,3},{3,4},{4,5},{5,6},{6,7},{7,8},{8,9},{9,10},{10,1... | collective-permute-start | bytes 147464 | tf_op jit(solution)/shard_map/ppermute | solution.py:15
  17.7 1.2 copy-start
  21.8 1.1 copy-start.3
  30.2 6.7 %collective-permute-start.3 = (bf16[6,16,256]{2,1,0:T(8,128)(2,1)S(1)}, bf16[6,16,256]{2,1,0:T(8,128)(2,1)S(1)}, u32[]{:S(2)}, u32[]{:S(2)}) collective-permute-start(bf16[6,16,256]{2,1,0:T(8,128)(2,1)S(1)} %get-tuple-element.11), channel_id=1, source_target_pairs={{1,0},{2,1},{3,2},{4,3},{5,4},{6,5},{7,6},{8,7},{9,8},{10,9},{11,1... | collective-permute-start | bytes 147464 | tf_op jit(solution)/shard_map/ppermute | solution.py:15
  31.5 6.0 %collective-permute-start.2 = (bf16[6,16,256]{2,1,0:T(8,128)(2,1)S(1)}, bf16[6,16,256]{2,1,0:T(8,128)(2,1)S(1)}, u32[]{:S(2)}, u32[]{:S(2)}) collective-permute-start(bf16[6,16,256]{2,1,0:T(8,128)(2,1)S(1)} %get-tuple-element.12), channel_id=1, source_target_pairs={{0,1},{1,2},{2,3},{3,4},{4,5},{5,6},{6,7},{7,8},{8,9},{9,10},{10,1... | collective-permute-start | bytes 147464 | tf_op jit(solution)/shard_map/ppermute | solution.py:15
  41.5 1.3 copy-start.2
Sparse Core Ops, SparseCore 0:
  30.4 102.8 all-reduce.1
where the time goes:
time: 144 us; the launch traced here: 143 us
  waiting for transfers between devices  88.1 us (61%)
  between operations  14.4 us (10%)
  starting transfers between devices  11 us (8%)
  other arithmetic  10.2 us (7%)
  matrix products  10 us (7%)
  local copies, waits for them, and re-layouts  9.6 us (7%)
    psum x1, waiting for transfers between devices, body(): summed = lax.psum(weight_part, 'tile')  87.5 us
    ppermute x4, starting transfers between devices, from_behind(): lax.ppermute(value, axis, [(source, source + steps) for source in range(i...  10.9 us
    unnamed x24, local copies, waits for them, and re-layouts  5.97 us
    dot_general x1, matrix products, forward_tiles(): jnp.dot(tap_matrix(extended, False), weight_mat, preferred_element_type=j...  3.56 us
    dot_general x1, matrix products, weight_terms(): lax.dot_general(tap_matrix(ext_x, False), slope_map.reshape(-1, slope_map...  3.52 us
    mul x1, other arithmetic, body(): weight_grad = (summed * grad_scale).reshape(9, channels, channels)  3.27 us
    dot_general x1, matrix products, backward_tiles(): jnp.dot(tap_matrix(ext_g, True), flip_mat, preferred_element_type=jnp.flo...  2.96 us
  transfers between devices with their start and end apart: 5, of which 2 were waited for; matrix products, arithmetic and copies ran while one was open for 9% of the time, Pallas kernels for 0%

commit v1 on v0

--- a/solution.py
+++ b/solution.py
@@ -7,6 +7,18 @@
 EDGE_PICK = (1, 0, 3, 2, 1, 1, 0, 0)
 ROOT_HALF = 0.7071067811865476
 INV_ROOT_TAU = 0.3989422804014327
+
+
+def expand_the_core(state):
+    mesh_name = "tile"
+    fan = lax.axis_size(mesh_name)
+    r_now = state
+    for i0 in [ix for ix in (1, 2, 4, 8, 16) if ix < fan]:
+        made = []
+        for hop_no in tuple(range(fan)):
+            made.append((hop_no, hop_no ^ i0))
+        r_now = r_now + lax.ppermute(r_now, axis_name=mesh_name, perm=made)
+    return r_now
 
 
 def from_behind(value, axis, steps):
@@ -140,7 +152,7 @@
     ext_g = surround(pre_grad, lookup(table_g, source, linked))
     weight_part = weight_terms(ext_x, pre_grad)
     grad_scale = 1.0 / math.sqrt(tile_dev * devices * side_cells * side_cells)
-    summed = lax.psum(weight_part, "tile")
+    summed = expand_the_core(weight_part)
     weight_grad = (summed * grad_scale).reshape(9, channels, channels)
     input_grad = backward_tiles(ext_g, tissue, flip_mat)
     return (activation, weight_grad, input_grad)

time: 144 us -> 243 us (1.69)
  waiting for transfers between devices: 88.1 us -> 191 us
  between operations: 14.4 us -> 1.05 us
  starting transfers between devices: 11 us -> 18.2 us
    ppermute x0 -> x4, waiting for transfers between devices: none -> 191 us  [expand_the_core(): r_now = r_now + lax.ppermute(r_now, axis_name=mesh_name, perm=made)]
    psum x1 -> x0, waiting for transfers between devices: 87.5 us -> none  [body(): summed = lax.psum(weight_part, 'tile')]
    ppermute x0 -> x4, starting transfers between devices: none -> 9.37 us  [expand_the_core(): r_now = r_now + lax.ppermute(r_now, axis_name=mesh_name, perm=made)]
    add x0 -> x3, other arithmetic: none -> 2.57 us  [expand_the_core(): r_now = r_now + lax.ppermute(r_now, axis_name=mesh_name, perm=made)]
  transfers between devices with their start and end apart: 5 -> 8, of which waited for: 2 -> 5; matrix products, arithmetic and copies ran while one was open for 9% -> 6% of each run, Pallas kernels for 0% -> 0%
where the time goes in v1:
time: 243 us
  waiting for transfers between devices  191 us (79%)
  starting transfers between devices  18.2 us (7%)
  other arithmetic  12.2 us (5%)
  local copies, waits for them, and re-layouts  11.4 us (5%)
  matrix products  8.66 us (4%)
    ppermute x4, waiting for transfers between devices, expand_the_core(): r_now = r_now + lax.ppermute(r_now, axis_name=mesh_name, perm=made)  191 us
    ppermute x4, starting transfers between devices, expand_the_core(): r_now = r_now + lax.ppermute(r_now, axis_name=mesh_name, perm=made)  9.37 us
    ppermute x4, starting transfers between devices, from_behind(): lax.ppermute(value, axis, [(source, source + steps) for source in range(i...  8.83 us
    unnamed x24, local copies, waits for them, and re-layouts  7.04 us
  transfers between devices with their start and end apart: 8, of which 5 were waited for; matrix products, arithmetic and copies ran while one was open for 6% of the time, Pallas kernels for 0%

profile of v1, /device:TPU:0, one launch (start us, length us, event | category | flops | bytes accessed | tf_op | source)
XLA Modules:
  0.0 242.8 jit_solution(3070552431671371544)
XLA Ops:
  0.6 0.8 slice_bitcast_fusion.11
  1.5 1.3 collective-permute-start.1
  2.8 3.0 %collective-permute-start = (bf16[6,16,256]{2,1,0:T(8,128)(2,1)S(1)}, bf16[6,16,256]{2,1,0:T(8,128)(2,1)S(1)}, u32[]{:S(2)}, u32[]{:S(2)}) collective-permute-start(bf16[6,16,256]{2,1,0:T(8,128)(2,1)S(1)} %get-tuple-element.18), channel_id=1, source_target_pairs={{0,1},{1,2},{2,3},{3,4},{4,5},{5,6},{6,7},{7,8},{8,9},{9,10},{10,1... | collective-permute-start | bytes 147464 | tf_op jit(solution)/shard_map/ppermute | solution.py:27
  5.8 1.3 fusion.14
  7.1 0.7 select_clamp_fusion
  7.8 0.1 reshape.50
  7.9 0.7 broadcast_compare_fusion
  8.6 0.7 compare_convert_fusion
  9.3 0.0 copy-start
  9.4 0.1 copy.60
  9.5 0.6 gather_fusion
  10.1 0.1 broadcast_select_fusion.1
  10.2 0.1 copy_select_fusion.1
  10.4 0.1 copy.70
  10.5 0.1 copy.69
  10.7 1.2 pad_maximum_fusion
  11.9 0.1 slice_dynamic-update-slice_fusion.11
  12.0 0.3 slice_dynamic-update-slice_fusion.10
  12.3 0.3 slice_dynamic-update-slice_fusion.9
  12.6 0.4 fusion.10
  13.0 0.1 constant_dynamic-update-slice_fusion
  13.1 0.5 fusion.9
  13.6 0.0 copy-start.3
  13.6 0.1 slice_dynamic-update-slice_fusion.8
  13.7 0.3 slice_dynamic-update-slice_fusion.7
  14.0 0.3 slice_dynamic-update-slice_fusion.6
  14.3 0.5 copy-done.1
  14.8 0.2 copy-done.3
  15.0 3.6 %fusion.6 = (bf16[6,16,16,256]{3,2,1,0:T(8,128)(2,1)S(1)}, bf16[6,16,16,256]{3,2,1,0:T(8,128)(2,1)}) fusion(bf16[6,16,16,256]{3,2,1,0:T(8,128)(2,1)S(1)} %copy-done.3, f32[6]{0:T(128)S(1)} %compare_convert_fusion, bf16[6,16,16,2304]{3,2,1,0:T(8,128)(2,1)S(1)} %slice_dynamic-update-slice_fusion.6, bf16[2304,256,1,1]{1,0,3,2:T(8,128)(2,1)S(1)} %bitcast.104), kind=kOutput, calls=%fused_computation.11 | convolution fusion | flops 1817837568 | bytes 10616856 | tf_op jit(solution)/shard_map/dot_general | solution.py:100
  18.6 2.1 convolution_bitcast_fusion
  20.8 2.6 %collective-permute-start.2 = (f32[2304,256]{1,0:T(8,128)S(1)}, f32[2304,256]{1,0:T(8,128)S(1)}, u32[]{:S(2)}, u32[]{:S(2)}) collective-permute-start(f32[2304,256]{1,0:T(8,128)S(1)} %convolution_bitcast_fusion), channel_id=1, source_target_pairs={{0,1},{1,0},{2,3},{3,2},{4,5},{5,4},{6,7},{7,6},{8,9},{9,8},{10,11... | collective-permute-start | bytes 7077896 | tf_op jit(solution)/shard_map/ppermute | solution.py:20
  23.4 4.2 %collective-permute-done.2 = f32[2304,256]{1,0:T(8,128)S(1)} collective-permute-done((f32[2304,256]{1,0:T(8,128)S(1)}, f32[2304,256]{1,0:T(8,128)S(1)}, u32[]{:S(2)}, u32[]{:S(2)}) %collective-permute-start.2) | collective-permute-done | bytes 2359328 | tf_op jit(solution)/shard_map/ppermute | solution.py:20
  27.6 0.3 add.55
  27.9 2.4 collective-permute-start.3
  30.3 51.8 %collective-permute-done.3 = f32[2304,256]{1,0:T(8,128)S(1)} collective-permute-done((f32[2304,256]{1,0:T(8,128)S(1)}, f32[2304,256]{1,0:T(8,128)S(1)}, u32[]{:S(2)}, u32[]{:S(2)}) %collective-permute-start.3) | collective-permute-done | bytes 2359328 | tf_op jit(solution)/shard_map/ppermute | solution.py:20
  82.1 0.3 add.56
  82.4 1.6 collective-permute-start.4
  84.0 2.4 copy.89
  86.4 1.3 collective-permute-start.7
  87.7 3.2 %collective-permute-start.6 = (bf16[6,16,256]{2,1,0:T(8,128)(2,1)S(1)}, bf16[6,16,256]{2,1,0:T(8,128)(2,1)S(1)}, u32[]{:S(2)}, u32[]{:S(2)}) collective-permute-start(bf16[6,16,256]{2,1,0:T(8,128)(2,1)S(1)} %get-tuple-element.12), channel_id=1, source_target_pairs={{0,1},{1,2},{2,3},{3,4},{4,5},{5,6},{6,7},{7,8},{8,9},{9,10},{10,1... | collective-permute-start | bytes 147464 | tf_op jit(solution)/shard_map/ppermute | solution.py:27
  90.9 0.2 fusion.13
  91.2 0.4 collective-permute-done.6
  91.7 1.3 gather_fusion.1
  93.0 1.1 broadcast_select_fusion
  94.1 0.1 copy_select_fusion
  94.3 0.1 copy.80
  94.3 0.1 copy.79
  94.5 1.2 maximum_maximum_fusion.1
  95.7 39.8 %collective-permute-done.4 = f32[2304,256]{1,0:T(8,128)} collective-permute-done((f32[2304,256]{1,0:T(8,128)S(1)}, f32[2304,256]{1,0:T(8,128)}, u32[]{:S(2)}, u32[]{:S(2)}) %collective-permute-start.4) | collective-permute-done | bytes 2359328 | tf_op jit(solution)/shard_map/ppermute | solution.py:20
  135.5 2.0 add.57
  137.5 2.7 %collective-permute-start.5 = (f32[2304,256]{1,0:T(8,128)S(1)}, f32[2304,256]{1,0:T(8,128)S(1)}, u32[]{:S(2)}, u32[]{:S(2)}) collective-permute-start(f32[2304,256]{1,0:T(8,128)S(1)} %add.57), channel_id=1, source_target_pairs={{0,8},{1,9},{2,10},{3,11},{4,12},{5,13},{6,14},{7,15},{8,0},{9,1},... | collective-permute-start | bytes 7077896 | tf_op jit(solution)/shard_map/ppermute | solution.py:20
  140.1 0.3 slice_dynamic-update-slice_fusion.5
  140.4 0.3 slice_dynamic-update-slice_fusion.4
  140.7 0.1 slice_dynamic-update-slice_fusion.3
  140.8 0.5 fusion.8
  141.3 0.1 constant_dynamic-update-slice_fusion.1
  141.4 0.4 fusion.7
  141.7 0.3 slice_dynamic-update-slice_fusion.2
  142.1 0.3 slice_dynamic-update-slice_fusion.1
  142.4 0.1 slice_dynamic-update-slice_fusion
  142.5 0.5 copy-done.2
  143.0 3.0 %multiply_convert_fusion = bf16[6,16,16,256]{3,2,1,0:T(8,128)(2,1)} fusion(bf16[6,16,16,2304]{3,2,1,0:T(8,128)(2,1)S(1)} %slice_dynamic-update-slice_fusion, bf16[2304,256,1,1]{1,0,3,2:T(8,128)(2,1)S(1)} %bitcast.105, f32[6]{0:T(128)S(1)} %compare_convert_fusion), kind=kOutput, calls=%fused_computation.12 | convolution fusion | flops 1812725760 | bytes 9043992 | tf_op jit(solution)/shard_map/dot_general | solution.py:123
  146.0 95.1 %collective-permute-done.5 = f32[2304,256]{1,0:T(8,128)S(1)} collective-permute-done((f32[2304,256]{1,0:T(8,128)S(1)}, f32[2304,256]{1,0:T(8,128)S(1)}, u32[]{:S(2)}, u32[]{:S(2)}) %collective-permute-start.5) | collective-permute-done | bytes 2359328 | tf_op jit(solution)/shard_map/ppermute | solution.py:20
  241.1 1.7 add_multiply_fusion
  (26 shorter events, 0.5 us)
Async XLA Ops:
  1.5 8.0 %collective-permute-start.1 = (bf16[6,16,256]{2,1,0:T(8,128)(2,1)S(1)}, bf16[6,16,256]{2,1,0:T(8,128)(2,1)S(1)}, u32[]{:S(2)}, u32[]{:S(2)}) collective-permute-start(bf16[6,16,256]{2,1,0:T(8,128)(2,1)S(1)} %get-tuple-element.17), channel_id=1, source_target_pairs={{1,0},{2,1},{3,2},{4,3},{5,4},{6,5},{7,6},{8,7},{9,8},{10,9},{11,1... | collective-permute-start | bytes 147464 | tf_op jit(solution)/shard_map/ppermute | solution.py:27
  2.8 6.7 %collective-permute-start = (bf16[6,16,256]{2,1,0:T(8,128)(2,1)S(1)}, bf16[6,16,256]{2,1,0:T(8,128)(2,1)S(1)}, u32[]{:S(2)}, u32[]{:S(2)}) collective-permute-start(bf16[6,16,256]{2,1,0:T(8,128)(2,1)S(1)} %get-tuple-element.18), channel_id=1, source_target_pairs={{0,1},{1,2},{2,3},{3,4},{4,5},{5,6},{6,7},{7,8},{8,9},{9,10},{10,1... | collective-permute-start | bytes 147464 | tf_op jit(solution)/shard_map/ppermute | solution.py:27
  9.3 1.4 copy-start
  13.6 1.3 copy-start.1
  13.6 1.5 copy-start.3
  20.8 6.8 %collective-permute-start.2 = (f32[2304,256]{1,0:T(8,128)S(1)}, f32[2304,256]{1,0:T(8,128)S(1)}, u32[]{:S(2)}, u32[]{:S(2)}) collective-permute-start(f32[2304,256]{1,0:T(8,128)S(1)} %convolution_bitcast_fusion), channel_id=1, source_target_pairs={{0,1},{1,0},{2,3},{3,2},{4,5},{5,4},{6,7},{7,6},{8,9},{9,8},{10,11... | collective-permute-start | bytes 7077896 | tf_op jit(solution)/shard_map/ppermute | solution.py:20
  27.9 54.2 %collective-permute-start.3 = (f32[2304,256]{1,0:T(8,128)S(1)}, f32[2304,256]{1,0:T(8,128)S(1)}, u32[]{:S(2)}, u32[]{:S(2)}) collective-permute-start(f32[2304,256]{1,0:T(8,128)S(1)} %add.55), channel_id=1, source_target_pairs={{0,2},{1,3},{2,0},{3,1},{4,6},{5,7},{6,4},{7,5},{8,10},{9,11},{10,... | collective-permute-start | bytes 7077896 | tf_op jit(solution)/shard_map/ppermute | solution.py:20
  82.4 53.1 %collective-permute-start.4 = (f32[2304,256]{1,0:T(8,128)S(1)}, f32[2304,256]{1,0:T(8,128)}, u32[]{:S(2)}, u32[]{:S(2)}) collective-permute-start(f32[2304,256]{1,0:T(8,128)S(1)} %add.56), channel_id=1, source_target_pairs={{0,4},{1,5},{2,6},{3,7},{4,0},{5,1},{6,2},{7,3},{8,12},{9,13},{10,... | collective-permute-start | bytes 7077896 | tf_op jit(solution)/shard_map/ppermute | solution.py:20
  86.4 4.8 %collective-permute-start.7 = (bf16[6,16,256]{2,1,0:T(8,128)(2,1)S(1)}, bf16[6,16,256]{2,1,0:T(8,128)(2,1)S(1)}, u32[]{:S(2)}, u32[]{:S(2)}) collective-permute-start(bf16[6,16,256]{2,1,0:T(8,128)(2,1)S(1)} %get-tuple-element.11), channel_id=1, source_target_pairs={{1,0},{2,1},{3,2},{4,3},{5,4},{6,5},{7,6},{8,7},{9,8},{10,9},{11,1... | collective-permute-start | bytes 147464 | tf_op jit(solution)/shard_map/ppermute | solution.py:27
  87.7 3.9 %collective-permute-start.6 = (bf16[6,16,256]{2,1,0:T(8,128)(2,1)S(1)}, bf16[6,16,256]{2,1,0:T(8,128)(2,1)S(1)}, u32[]{:S(2)}, u32[]{:S(2)}) collective-permute-start(bf16[6,16,256]{2,1,0:T(8,128)(2,1)S(1)} %get-tuple-element.12), channel_id=1, source_target_pairs={{0,1},{1,2},{2,3},{3,4},{4,5},{5,6},{6,7},{7,8},{8,9},{9,10},{10,1... | collective-permute-start | bytes 147464 | tf_op jit(solution)/shard_map/ppermute | solution.py:27
  137.5 103.6 %collective-permute-start.5 = (f32[2304,256]{1,0:T(8,128)S(1)}, f32[2304,256]{1,0:T(8,128)S(1)}, u32[]{:S(2)}, u32[]{:S(2)}) collective-permute-start(f32[2304,256]{1,0:T(8,128)S(1)} %add.57), channel_id=1, source_target_pairs={{0,8},{1,9},{2,10},{3,11},{4,12},{5,13},{6,14},{7,15},{8,0},{9,1},... | collective-permute-start | bytes 7077896 | tf_op jit(solution)/shard_map/ppermute | solution.py:20
  141.7 1.3 copy-start.2
